TPU v7x, 128 devices: a whole 4x4x4 slice. The times are simulated.
128 devices in a mesh: ctx: 32 (over z, y_lo, x), head: 4 (over y_hi, core).
Axes of the slice: x: 4, y: 4 (y_hi: 2, y_lo: 2; y = y_hi * 2 + y_lo), z: 4, core: 2. Of those that a mesh axis runs over, the one named last changes fastest.
Arguments:
- events: bfloat16 [24576, 1024], P('ctx', 'head'), may hold values from -3 to 3
- norm_gain: float32 [1024], replicated, may hold values from 0.5 to 1.5
- w_uvqk: bfloat16 [1024, 4, 1024], P(None, None, 'head'), may hold values from -4 to 4
- w_out: bfloat16 [1024, 1024], P('head'), may hold values from -0.1875 to 0.1875
- lengths: int32 [8], replicated, may hold values from 1 to 13824, 24576 in all
Outputs:
- mixed: bfloat16 [24576, 1024], P('ctx', 'head')
Inputs may be any that keep to these rules, and one draw needn't show every extreme that they name: The lengths sum to 24576; the longest is exactly 13824.
All inputs are finite; a program needn't handle non-finite values.
Results may differ from a plain program's by a relative error of at most 0.0062.
Values may be sent and summed in bfloat16 or wider, within the bound.
No kernel may reach another device: no remote copies, remote signals or barrier semaphores. Data moves between devices by JAX's collectives and lax.ppermute only.
A program may use at most 128 MiB of HBM per device.

v0:
```python
import jax
import jax.numpy as jnp
from jax import lax
from jax.sharding import PartitionSpec as P

D = 1024
HDIM = 128


def attend(totals, key_block, value_block, offset, queries, query_pos, query_seg, seq_ends):
    count = key_block.shape[0]
    key_pos = offset + jnp.arange(count, dtype=jnp.int32)
    key_seg = jnp.sum((key_pos[:, None] >= seq_ends[None, :]).astype(jnp.int32), axis=1)
    score_scale = key_block.shape[-1] ** (-0.5)
    scores = (
        jnp.einsum("qhd,khd->hqk", queries, key_block, preferred_element_type=jnp.float32)
        * score_scale
    )
    allowed = (
        (query_seg[:, None] == key_seg[None, :])
        & (key_pos[None, :] <= query_pos[:, None])
        & (key_pos[None, :] >= 0)
    )
    weights = jnp.where(allowed[None], jax.nn.silu(scores), 0.0).astype(jnp.bfloat16)
    return totals + jnp.einsum(
        "hqk,khd->qhd", weights, value_block, preferred_element_type=jnp.float32
    )


def shards(events, norm_gain, w_uvqk, w_out, lengths):
    epsilon = 1e-05
    row_count = events.shape[0]
    gathered = lax.all_gather(events, "head", axis=1, tiled=True)
    xfloat = gathered.astype(jnp.float32)
    row_mean = jnp.mean(xfloat, axis=-1, keepdims=True)
    centered = xfloat - row_mean
    row_var = jnp.mean(centered * centered, axis=-1, keepdims=True)
    normed = (centered * lax.rsqrt(row_var + epsilon) * norm_gain).astype(jnp.bfloat16)
    local_cols = w_uvqk.shape[2]
    heads_here = local_cols // HDIM
    projected = jax.nn.silu(
        jnp.dot(
            normed,
            w_uvqk.reshape(w_uvqk.shape[0], 4 * local_cols),
            preferred_element_type=jnp.float32,
        )
    ).astype(jnp.bfloat16)
    projected = projected.reshape(row_count, 4, heads_here, HDIM)
    gate_rows = projected[:, 0]
    value_rows = projected[:, 1]
    queries = projected[:, 2]
    key_rows = projected[:, 3]
    seq_ends = jnp.cumsum(lengths)
    seq_starts = seq_ends - lengths
    seq_index = jnp.arange(lengths.shape[0], dtype=jnp.int32)
    my_first = lax.axis_index("ctx") * row_count
    query_pos = my_first + jnp.arange(row_count, dtype=jnp.int32)
    query_seg = jnp.sum((query_pos[:, None] >= seq_ends[None, :]).astype(jnp.int32), axis=1)
    empty = jnp.zeros((row_count, heads_here, HDIM), jnp.float32)
    history_start = jnp.sum(jnp.where(query_seg[0] == seq_index, seq_starts, 0))
    last_row = my_first + row_count - 1
    key_all = lax.all_gather(key_rows, "ctx", axis=0, tiled=True)
    value_all = lax.all_gather(value_rows, "ctx", axis=0, tiled=True)
    block_rows = min(key_all.shape[0], row_count)
    turns = key_all.shape[0] // block_rows

    def inner(turn_index, running):
        lower = turn_index * block_rows
        key_block = lax.dynamic_slice_in_dim(key_all, lower, block_rows, 0)
        value_block = lax.dynamic_slice_in_dim(value_all, lower, block_rows, 0)
        needed = (lower + block_rows > history_start) & (lower <= last_row)

        def take_block(current):
            return attend(
                current, key_block, value_block, lower, queries, query_pos, query_seg, seq_ends
            )

        def skip_block(current):
            return current

        return lax.cond(needed, take_block, skip_block, running)

    attended = lax.fori_loop(0, turns, inner, empty)
    local_squares = jnp.sum(attended * attended, axis=(1, 2))
    squares = lax.psum(local_squares, "head")
    inverse_rms = lax.rsqrt(squares / D + epsilon)
    gated = (
        (attended * inverse_rms[:, None, None] * gate_rows.astype(jnp.float32))
        .astype(jnp.bfloat16)
        .reshape(row_count, local_cols)
    )
    partial_out = jnp.dot(gated, w_out, preferred_element_type=jnp.float32)
    shared = lax.psum_scatter(partial_out, "head", scatter_dimension=1, tiled=True)
    return (events.astype(jnp.float32) + shared).astype(jnp.bfloat16)


def solution(mesh):
    in_specs = (P("ctx", "head"), P(), P(None, None, "head"), P("head", None), P())
    out_specs = P("ctx", "head")
    return jax.shard_map(shards, mesh=mesh, in_specs=in_specs, out_specs=out_specs, check_vma=False)
```

profile of v0, /device:TPU:1, one launch (start us, length us, event | category | flops | bytes accessed | tf_op | source)
XLA Modules:
  0.0 572.1 jit_solution(18329584764954480928)
XLA Ops:
  6.5 0.0 copy-start
  6.5 0.0 all-gather.6.cloned.1.call-start
  6.5 0.7 all-gather.6.cloned.1.call-update
  7.3 0.0 all-gather.8.cloned.1.call-start
  7.3 0.0 copy-start.4
  7.3 2.1 copy.28
  9.4 27.1 %all-gather.6.cloned.1.call-done = bf16[768,1024]{1,0:T(8,128)(2,1)} async-done(((bf16[768,256]{1,0:T(8,128)(2,1)}), bf16[768,1024]{1,0:T(8,128)(2,1)}) %all-gather.6.cloned.1.call-update) | async-done | bytes 1572880 | tf_op jit(solution)/shard_map/all_gather | solution.py:33
  36.5 0.0 copy-start.1
  36.5 1.8 convert_reduce_fusion.1
  38.3 2.0 fusion.27
  40.3 0.0 copy-done.4
  40.3 0.0 copy-done.1
  40.3 3.4 multiply_convert_fusion
  43.7 2.8 reshape.139
  46.5 0.0 copy-start.3
  46.5 1.1 fusion.39
  47.6 0.8 copy.24
  48.4 0.0 all-gather.8.cloned.1.call-update
  48.5 0.0 all-gather.10.cloned.1.call-start
  48.5 0.8 copy.26
  49.3 0.0 all-gather.10.cloned.1.call-update
  49.4 0.0 reduce-scatter.2.cloned.1.call-start
  49.4 0.0 copy-done.3
  49.4 0.2 reduce-window.8
  49.6 0.1 convert_reduce_fusion.2
  49.7 0.5 slice.15
  50.2 1.3 fusion.38
  51.6 0.4 copy.27
  52.0 0.1 copy.30
  52.1 152.2 %all-gather.8.cloned.1.call-done = bf16[24576,1,2,128]{3,0,2,1:T(8,128)(2,1)} async-done(((bf16[768,1,2,128]{3,0,2,1:T(8,128)(2,1)}), bf16[24576,1,2,128]{3,0,2,1:T(8,128)(2,1)}) %all-gather.8.cloned.1.call-update) | async-done | bytes 12582928 | tf_op jit(solution)/shard_map/all_gather | solution.py:62
  204.2 175.0 %all-gather.10.cloned.1.call-done = bf16[24576,1,2,128]{3,0,2,1:T(8,128)(2,1)} async-done(((bf16[768,1,2,128]{3,0,2,1:T(8,128)(2,1)}), bf16[24576,1,2,128]{3,0,2,1:T(8,128)(2,1)}) %all-gather.10.cloned.1.call-update) | async-done | bytes 12582928 | tf_op jit(solution)/shard_map/all_gather | solution.py:63
  379.3 0.1 broadcast_in_dim.40
  379.3 28.9 %while.17 = (s32[]{:T(128)}, f32[768,2,128]{2,0,1:T(8,128)S(1)}, s32[]{:T(128)}, s32[]{:T(128)}, s32[768]{0:T(1024)S(1)}, /*index=5*/s32[8]{0:T(128)S(1)}, bf16[...) while((s32[]{:T(128)}, f32[768,2,128]{2,0,1:T(8,128)S(1)}, ...), condition=%wide.region_9.10_spmd.clone, body=%wide.region_5.9_spmd.clone.sunk | while | flops 614813952 | bytes 3965765 | solution.py:83
  380.0 4.9 conditional.3
  380.1 0.1 convert_reduce_fusion
  380.2 0.8 and_and_fusion
  381.0 3.9 fusion.14
  408.2 0.2 multiply_reduce_fusion
  408.4 0.3 copy.21
  408.7 25.6 %psum.7 = f32[768]{0:T(1024)S(1)} all-reduce(f32[768]{0:T(1024)S(1)} %multiply_reduce_fusion), channel_id=1, replica_groups=mesh['ctx'=32,'head'=4] {'head'}, use_global_device_ids=true, to_apply=%region_11.12 | all-reduce | flops 768 | bytes 6144 | tf_op jit(solution)/shard_map/psum | solution.py:85
  434.3 0.1 fusion.37
  434.4 0.0 copy-done
  434.4 0.0 copy-start.2
  434.4 2.3 fusion.40
  436.7 0.0 reduce-scatter.2.cloned.1.call-update
  436.7 126.9 %reduce-scatter.2.cloned.1.call-done = f32[768,256]{1,0:T(8,128)} async-done(((f32[768,1024]{1,0:T(8,128)}), f32[768,256]{1,0:T(8,128)}) %reduce-scatter.2.cloned.1.call-update) | async-done | bytes 786448 | tf_op jit(solution)/shard_map/reduce_scatter | solution.py:93
  563.6 0.0 copy-done.2
  563.6 2.0 add_convert_fusion
  (69 shorter events, 0.7 us)
Async XLA Ops:
  6.5 427.8 %copy-start = (bf16[256,1024]{1,0:T(8,128)(2,1)S(1)}, bf16[256,1024]{1,0:T(8,128)(2,1)}, u32[]{:S(2)}) copy-start(bf16[256,1024]{1,0:T(8,128)(2,1)} %param.12) | copy-start | bytes 1572868
  6.5 30.0 %all-gather.6.cloned.1.call-start = ((), (), s32[]{:S(2)}) async-start(), calls=%async_computation.1 | async-start | bytes 1966080 | tf_op jit(solution)/shard_map/all_gather | solution.py:33
  7.3 197.0 %all-gather.8.cloned.1.call-start = ((), (), s32[]{:S(2)}) async-start(), calls=%async_computation.3 | async-start | bytes 12976128 | tf_op jit(solution)/shard_map/all_gather | solution.py:62
  7.3 33.0 %copy-start.4 = (f32[1024]{0:T(1024)S(1)}, f32[1024]{0:T(1024)}, u32[]{:S(2)}) copy-start(f32[1024]{0:T(1024)} %param.10) | copy-start | bytes 12292
  36.5 3.8 copy-start.1
  46.5 2.9 copy-start.3
  48.5 330.8 %all-gather.10.cloned.1.call-start = ((), (), s32[]{:S(2)}) async-start(), calls=%async_computation.4 | async-start | bytes 12976128 | tf_op jit(solution)/shard_map/all_gather | solution.py:63
  49.4 514.2 %reduce-scatter.2.cloned.1.call-start = ((), (), s32[]{:S(2)}) async-start(), calls=%async_computation.2 | async-start | bytes 3932160 | tf_op jit(solution)/shard_map/reduce_scatter | solution.py:93
  434.4 129.2 %copy-start.2 = (bf16[768,256]{1,0:T(8,128)(2,1)S(1)}, bf16[768,256]{1,0:T(8,128)(2,1)}, u32[]{:S(2)}) copy-start(bf16[768,256]{1,0:T(8,128)(2,1)} %param.9) | copy-start | bytes 1179652
Sparse Core Ops, SparseCore 0:
  9.0 27.4 all-gather.5
  48.6 155.6 all-gather.7
  205.9 173.3 all-gather.9
  436.8 126.7 reduce-scatter.1
where the time goes:
time: 573 us; the launch traced here: 572 us
  waiting for transfers between devices  482 us (84%)
  blocking collectives  25.6 us (4%)
  loops' own time  23.9 us (4%)
  between operations  13.3 us (2%)
  matrix products  9.58 us (2%)
  local copies, waits for them, and re-layouts  9.07 us (2%)
  other arithmetic  8.59 us (1%)
    all_gather x1, waiting for transfers between devices, shards(): value_all = lax.all_gather(value_rows, 'ctx', axis=0, tiled=True)  175 us
    all_gather x1, waiting for transfers between devices, shards(): key_all = lax.all_gather(key_rows, 'ctx', axis=0, tiled=True)  152 us
    reduce_scatter x1, waiting for transfers between devices, shards(): lax.psum_scatter(partial_out, 'head', scatter_dimension=1, tiled=True)  127 us
    all_gather x1, waiting for transfers between devices, shards(): gathered = lax.all_gather(events, 'head', axis=1, tiled=True)  27.1 us
    psum x1, blocking collectives, shards(): squares = lax.psum(local_squares, 'head')  25.6 us
    another operation x1, loops' own time, shards(): attended = lax.fori_loop(0, turns, inner, empty)  23.3 us
  transfers between devices with their start and end apart: 4, of which 4 were waited for; matrix products, arithmetic and copies ran while one was open for 1% of the time, Pallas kernels for 0%

commit v1 on v0

--- a/solution.py
+++ b/solution.py
@@ -28,6 +28,12 @@
 
 
 def shards(events, norm_gain, w_uvqk, w_out, lengths):
+
+    def do_zones(array_in, payload, bus_axis):
+        field_out = jnp.concatenate([array_in, payload], axis=1)
+        v_next = jax.lax.all_gather(field_out, bus_axis, axis=0, tiled=True)
+        return jnp.split(v_next, [array_in.shape[1]], axis=1)
+
     epsilon = 1e-05
     row_count = events.shape[0]
     gathered = lax.all_gather(events, "head", axis=1, tiled=True)
@@ -59,8 +65,7 @@
     empty = jnp.zeros((row_count, heads_here, HDIM), jnp.float32)
     history_start = jnp.sum(jnp.where(query_seg[0] == seq_index, seq_starts, 0))
     last_row = my_first + row_count - 1
-    key_all = lax.all_gather(key_rows, "ctx", axis=0, tiled=True)
-    value_all = lax.all_gather(value_rows, "ctx", axis=0, tiled=True)
+    key_all, value_all = do_zones(key_rows, value_rows, "ctx")
     block_rows = min(key_all.shape[0], row_count)
     turns = key_all.shape[0] // block_rows
 

time: 573 us -> 518 us (0.904)
  waiting for transfers between devices: 482 us -> 430 us
  blocking collectives: 25.6 us -> 7.37 us
  local copies, waits for them, and re-layouts: 9.07 us -> 24.5 us
    all_gather x2 -> x1, waiting for transfers between devices: 327 us -> 274 us  [do_zones(): v_next = jax.lax.all_gather(field_out, bus_axis, axis=0, tiled=True)]
    psum x1, blocking collectives: 25.6 us -> 7.37 us  [shards(): squares = lax.psum(local_squares, 'head')]
    split x0 -> x1, local copies, waits for them, and re-layouts: none -> 16.9 us  [do_zones(): return jnp.split(v_next, [array_in.shape[1]], axis=1)]
  transfers between devices with their start and end apart: 4 -> 3, of which waited for: 4 -> 3; matrix products, arithmetic and copies ran while one was open for 1% -> 1% of each run, Pallas kernels for 0% -> 0%
where the time goes in v1:
time: 518 us; the launch traced here: 517 us
  waiting for transfers between devices  430 us (83%)
  local copies, waits for them, and re-layouts  24.5 us (5%)
  loops' own time  23.5 us (5%)
  between operations  13.3 us (3%)
  matrix products  9.55 us (2%)
  other arithmetic  9.54 us (2%)
  blocking collectives  7.37 us (1%)
    all_gather x1, waiting for transfers between devices, do_zones(): v_next = jax.lax.all_gather(field_out, bus_axis, axis=0, tiled=True)  274 us
    reduce_scatter x1, waiting for transfers between devices, shards(): lax.psum_scatter(partial_out, 'head', scatter_dimension=1, tiled=True)  128 us
    all_gather x1, waiting for transfers between devices, shards(): gathered = lax.all_gather(events, 'head', axis=1, tiled=True)  27.1 us
    another operation x1, loops' own time, shards(): attended = lax.fori_loop(0, turns, inner, empty)  23 us
    split x1, local copies, waits for them, and re-layouts, do_zones(): return jnp.split(v_next, [array_in.shape[1]], axis=1)  16.9 us
  transfers between devices with their start and end apart: 3, of which 3 were waited for; matrix products, arithmetic and copies ran while one was open for 1% of the time, Pallas kernels for 0%

profile of v1, /device:TPU:1, one launch (start us, length us, event | category | flops | bytes accessed | tf_op | source)
XLA Modules:
  0.0 517.4 jit_solution(5259224613004817962)
XLA Ops:
  6.5 0.0 copy-start
  6.5 0.0 all-gather.3.cloned.1.call-start
  6.5 0.7 all-gather.3.cloned.1.call-update
  7.3 0.0 all-gather.5.cloned.1.call-start
  7.3 0.0 copy-start.4
  7.3 2.1 copy.28
  9.4 27.1 %all-gather.3.cloned.1.call-done = bf16[768,1024]{1,0:T(8,128)(2,1)} async-done(((bf16[768,256]{1,0:T(8,128)(2,1)}), bf16[768,1024]{1,0:T(8,128)(2,1)}) %all-gather.3.cloned.1.call-update) | async-done | bytes 1572880 | tf_op jit(solution)/shard_map/all_gather | solution.py:39
  36.5 0.0 copy-start.1
  36.5 1.8 convert_reduce_fusion.1
  38.3 2.0 fusion.27
  40.3 0.0 copy-done.4
  40.3 0.0 copy-done.1
  40.3 3.4 multiply_convert_fusion
  43.7 2.8 reshape.139
  46.5 0.0 copy-start.3
  46.5 1.1 fusion.40
  47.6 0.1 copy_bitcast_fusion.1
  47.7 1.0 pad_maximum_fusion
  48.7 0.0 all-gather.5.cloned.1.call-update
  48.8 0.0 reduce-scatter.2.cloned.1.call-start
  48.8 0.0 copy-done.3
  48.8 0.2 reduce-window.8
  49.0 0.1 convert_reduce_fusion.2
  49.1 0.5 slice.15
  49.7 1.3 fusion.38
  51.0 0.1 copy.32
  51.0 0.4 copy.27
  51.5 274.0 %all-gather.5.cloned.1.call-done = bf16[24576,4,128]{2,0,1:T(8,128)(2,1)} async-done(((bf16[768,4,128]{2,0,1:T(8,128)(2,1)}), bf16[24576,4,128]{2,0,1:T(8,128)(2,1)}) %all-gather.5.cloned.1.call-update) | async-done | bytes 25165840 | tf_op jit(solution)/shard_map/all_gather | solution.py:34
  325.5 16.9 %fusion.39 = (bf16[24576,2,128]{2,0,1:T(8,128)(2,1)}, bf16[24576,2,128]{2,0,1:T(8,128)(2,1)}) fusion(bf16[24576,4,128]{2,0,1:T(8,128)(2,1)} %all-gather.5.cloned.1.call-done), kind=kLoop, calls=%fused_computation.50 | loop fusion | bytes 50331648 | tf_op jit(solution)/shard_map/split | solution.py:35
  342.4 0.1 broadcast_in_dim.40
  342.5 28.4 %while.17 = (s32[]{:T(128)}, f32[768,2,128]{2,0,1:T(8,128)S(1)}, s32[]{:T(128)}, s32[]{:T(128)}, s32[768]{0:T(1024)S(1)}, /*index=5*/s32[8]{0:T(128)S(1)}, bf16[...) while((s32[]{:T(128)}, f32[768,2,128]{2,0,1:T(8,128)S(1)}, ...), condition=%wide.region_9.10_spmd.clone, body=%wide.region_5.9_spmd.clone.sunk | while | flops 614813952 | bytes 3965765 | solution.py:88
  343.2 4.9 conditional.3
  343.2 0.1 convert_reduce_fusion
  343.3 0.8 and_and_fusion
  344.2 3.9 fusion.14
  370.9 0.3 copy.21
  371.2 0.2 multiply_reduce_fusion
  371.3 7.4 %psum.7 = f32[768]{0:T(1024)S(1)} all-reduce(f32[768]{0:T(1024)S(1)} %multiply_reduce_fusion), channel_id=1, replica_groups=mesh['ctx'=32,'head'=4] {'head'}, use_global_device_ids=true, to_apply=%region_11.12 | all-reduce | flops 768 | bytes 6144 | tf_op jit(solution)/shard_map/psum | solution.py:90
  378.7 0.1 fusion.37
  378.8 0.0 copy-done
  378.8 0.0 copy-start.2
  378.8 2.3 fusion.41
  381.1 0.0 reduce-scatter.2.cloned.1.call-update
  381.1 127.7 %reduce-scatter.2.cloned.1.call-done = f32[768,256]{1,0:T(8,128)} async-done(((f32[768,1024]{1,0:T(8,128)}), f32[768,256]{1,0:T(8,128)}) %reduce-scatter.2.cloned.1.call-update) | async-done | bytes 786448 | tf_op jit(solution)/shard_map/reduce_scatter | solution.py:98
  508.9 0.0 copy-done.2
  508.9 2.0 add_convert_fusion
  (69 shorter events, 0.5 us)
Async XLA Ops:
  6.5 372.3 %copy-start = (bf16[256,1024]{1,0:T(8,128)(2,1)S(1)}, bf16[256,1024]{1,0:T(8,128)(2,1)}, u32[]{:S(2)}) copy-start(bf16[256,1024]{1,0:T(8,128)(2,1)} %param.12) | copy-start | bytes 1572868
  6.5 30.0 %all-gather.3.cloned.1.call-start = ((), (), s32[]{:S(2)}) async-start(), calls=%async_computation.1 | async-start | bytes 1966080 | tf_op jit(solution)/shard_map/all_gather | solution.py:39
  7.3 318.2 %all-gather.5.cloned.1.call-start = ((), (), s32[]{:S(2)}) async-start(), calls=%async_computation.2 | async-start | bytes 25952256 | tf_op jit(solution)/shard_map/all_gather | solution.py:34
  7.3 33.0 %copy-start.4 = (f32[1024]{0:T(1024)S(1)}, f32[1024]{0:T(1024)}, u32[]{:S(2)}) copy-start(f32[1024]{0:T(1024)} %param.10) | copy-start | bytes 12292
  36.5 3.8 copy-start.1
  46.5 2.3 copy-start.3
  48.8 460.1 %reduce-scatter.2.cloned.1.call-start = ((), (), s32[]{:S(2)}) async-start(), calls=%async_computation.3 | async-start | bytes 3932160 | tf_op jit(solution)/shard_map/reduce_scatter | solution.py:98
  378.8 130.0 %copy-start.2 = (bf16[768,256]{1,0:T(8,128)(2,1)S(1)}, bf16[768,256]{1,0:T(8,128)(2,1)}, u32[]{:S(2)}) copy-start(bf16[768,256]{1,0:T(8,128)(2,1)} %param.9) | copy-start | bytes 1179652
Sparse Core Ops, SparseCore 0:
  9.0 27.4 all-gather.2
  48.9 276.5 all-gather.4
  381.3 127.5 reduce-scatter.1
